TPU v7x, 256 devices: a whole 4x4x8 slice. The times are simulated.
256 devices in a mesh: tok: 64 (over x, z, core), ch: 4 (over y).
Axes of the slice: x: 4, y: 4, z: 8, core: 2. Of those that a mesh axis runs over, the one named last changes fastest.
Arguments:
- inputs: float32 [65536, 1024], P('tok', 'ch'), may hold values from -6 to 6
- factor_one: float32 [512, 512], replicated, may hold values from -0.25 to 0.25
- twiddle: float32 [128, 512], P('tok'), may hold values from -4 to 4
- factor_two: float32 [128, 128], replicated, may hold values from -0.5 to 0.5
- w_up: bfloat16 [4, 256, 1024], P('ch', 'tok'), may hold values from -0.375 to 0.375
- w_down: bfloat16 [4, 1024, 256], P('ch', 'tok'), may hold values from -0.1875 to 0.1875
- out_cotangent: float32 [65536, 1024], P('tok', 'ch'), may hold values from -6 to 6
Outputs:
- outputs: float32 [65536, 1024], P('tok', 'ch')
- grad_inputs: float32 [65536, 1024], P('tok', 'ch')
- grad_factor_one: float32 [512, 512], replicated
- grad_factor_two: float32 [128, 128], replicated
- grad_up: float32 [4, 256, 1024], P('ch', 'tok')
- grad_down: float32 [4, 1024, 256], P('ch', 'tok')
All inputs are finite; a program needn't handle non-finite values.
Results may differ from a plain program's by a relative error of at most 0.0057.
Values may be sent and summed in bfloat16 or wider, within the bound.
A program may use at most 64 MiB of HBM per device.

v0:
```python
import math
import jax
import jax.numpy as jnp
from jax import lax
from jax.sharding import PartitionSpec as P

inv_root_two = 1.0 / math.sqrt(2.0)
inv_root_tau = 1.0 / math.sqrt(2.0 * math.pi)


def gelu_parts(value):
    cdf = 0.5 * (1.0 + jax.scipy.special.erf(value * inv_root_two))
    return (value * cdf, cdf + value * jnp.exp(-0.5 * value * value) * inv_root_tau)


def to_columns(block):
    count = lax.axis_size("tok")
    rows, width, chans = block.shape
    return lax.all_to_all(
        block.reshape(rows, count, width // count, chans),
        "tok",
        split_axis=1,
        concat_axis=0,
        tiled=True,
    ).reshape(count * rows, width // count, chans)


def to_rows(block):
    return lax.all_to_all(block, "tok", split_axis=0, concat_axis=1, tiled=True)


def local(inputs, factor_one, twiddle, factor_two, w_up, w_down, out_cotangent):
    high = lax.Precision.HIGHEST
    rows = twiddle.shape[0]
    width = twiddle.shape[1]
    chans = inputs.shape[1]
    panels = (
        lax.all_gather(w_up, "tok", axis=1, tiled=True),
        lax.all_gather(w_down, "tok", axis=1, tiled=True),
    )
    up_w = panels[0][0]
    down_w = panels[1][0]
    grid = inputs.reshape(rows, width, chans)
    first = jnp.einsum("kj,ijc->ikc", factor_one, grid, precision=high)
    mid = first * twiddle[:, :, None]
    mid_cols = to_columns(mid)
    mixed_cols = jnp.einsum("mi,ikc->mkc", factor_two, mid_cols, precision=high)
    mixed = to_rows(mixed_cols).reshape(rows * width, chans)
    gate = jax.nn.sigmoid(inputs)
    branch = inputs + gate * mixed
    normed = branch.astype(jnp.bfloat16)
    up = jnp.dot(normed, up_w, preferred_element_type=jnp.float32)
    active, slope = gelu_parts(up)
    hidden = active.astype(jnp.bfloat16)
    outputs = branch + jnp.dot(hidden, down_w, preferred_element_type=jnp.float32)
    cot = out_cotangent.astype(jnp.bfloat16)
    d_hidden = jnp.dot(cot, down_w.T, preferred_element_type=jnp.float32)
    d_up = (d_hidden * slope).astype(jnp.bfloat16)
    d_branch = out_cotangent + jnp.dot(d_up, up_w.T, preferred_element_type=jnp.float32)
    grad_down_part = jnp.dot(hidden.T, cot, preferred_element_type=jnp.float32)
    grad_up_part = jnp.dot(normed.T, d_up, preferred_element_type=jnp.float32)
    grad_up, grad_down = (
        lax.psum_scatter(grad_up_part[None], "tok", scatter_dimension=1, tiled=True),
        lax.psum_scatter(grad_down_part[None], "tok", scatter_dimension=1, tiled=True),
    )
    d_mixed = d_branch * gate
    direct = d_branch * (1.0 + gate * (1.0 - gate) * mixed)
    cot_cols = to_columns(d_mixed.reshape(rows, width, chans))
    d_mid_cols = jnp.einsum("mi,mkc->ikc", factor_two, cot_cols, precision=high)
    two_part = jnp.einsum("mkc,ikc->mi", cot_cols, mid_cols, precision=high)
    d_first = to_rows(d_mid_cols) * twiddle[:, :, None]
    one_part = jnp.einsum("ikc,ijc->kj", d_first, grid, precision=high)
    d_grid = jnp.einsum("kj,ikc->ijc", factor_one, d_first, precision=high)
    grad_inputs = direct + d_grid.reshape(rows * width, chans)
    grad_one, grad_two = lax.psum((one_part, two_part), ("tok", "ch"))
    return (outputs, grad_inputs, grad_one, grad_two, grad_up, grad_down)


def solution(mesh):
    in_specs = (
        P("tok", "ch"),
        P(),
        P("tok", None),
        P(),
        P("ch", "tok", None),
        P("ch", "tok", None),
        P("tok", "ch"),
    )
    out_specs = (
        P("tok", "ch"),
        P("tok", "ch"),
        P(),
        P(),
        P("ch", "tok", None),
        P("ch", "tok", None),
    )
    return jax.shard_map(local, mesh=mesh, in_specs=in_specs, out_specs=out_specs, check_vma=False)
```

profile of v0, /device:TPU:4, one launch (start us, length us, event | category | flops | bytes accessed | tf_op | source)
XLA Modules:
  0.0 719.0 jit_solution(10194359381156684317)
XLA Ops:
  8.0 1.2 copy-done
  9.2 4.7 fusion.6
  14.5 38.7 %all_to_all.63 = f32[2,64,8,256]{3,2,0,1:T(8,128)S(1)} all-to-all(f32[2,64,8,256]{3,2,0,1:T(8,128)S(1)} %copy.66), channel_id=1, replica_groups=mesh['tok'=64,'ch'=4] {'tok'}, dimensions={1} | all-to-all | bytes 2097152 | tf_op jit(solution)/shard_map/all_to_all | solution.py:19
  53.1 1.0 copy-done.4
  54.1 1.9 convolution_bitcast_fusion.5
  56.0 1.4 copy.68
  57.4 8.1 %all-to-all-start.1 = ((f32[128,8,256]{2,1,0:T(8,128)}), f32[128,8,256]{2,1,0:T(8,128)S(1)}, u32[]{:S(2)}, u32[]{:S(2)}) async-start(f32[128,8,256]{2,1,0:T(8,128)} %copy.68), calls=%async_computation.1 | async-start | bytes 2097152 | tf_op jit(solution)/shard_map/all_to_all | solution.py:29
  65.6 72.8 %all_gather.6 = bf16[1,256,1024]{2,0,1:T(2,128)(2,1)} all-gather(bf16[1,4,1024]{2,0,1:T(2,128)(2,1)S(1)} %copy.70), channel_id=1, replica_groups=mesh['tok'=64,'ch'=4] {'tok'}, dimensions={1}, use_global_device_ids=true | all-gather | bytes 532480 | tf_op jit(solution)/shard_map/all_gather | solution.py:38
  138.4 53.1 %all_gather.7 = bf16[1,1024,256]{2,1,0:T(8,128)(2,1)} all-gather(bf16[1,16,256]{2,1,0:T(8,128)(2,1)S(1)} %copy-done.11), channel_id=1, replica_groups=mesh['tok'=64,'ch'=4] {'tok'}, dimensions={1}, use_global_device_ids=true | all-gather | bytes 532480 | tf_op jit(solution)/shard_map/all_gather | solution.py:39
  191.6 1.0 copy-done.2
  193.1 2.4 multiply_convert_fusion
  195.4 2.2 fusion.5
  197.6 1.8 fusion.33
  199.5 35.5 %all_to_all.64 = f32[2,64,8,256]{3,2,0,1:T(8,128)S(1)} all-to-all(f32[2,64,8,256]{3,2,0,1:T(8,128)S(1)} %copy.71), channel_id=1, replica_groups=mesh['tok'=64,'ch'=4] {'tok'}, dimensions={1} | all-to-all | bytes 2097152 | tf_op jit(solution)/shard_map/all_to_all | solution.py:19
  235.1 1.1 copy-done.5
  236.1 2.9 convolution_bitcast_fusion.4
  239.0 2.7 copy.73
  241.7 8.3 %all-to-all-start.3 = ((f32[128,8,256]{2,1,0:T(8,128)}), f32[128,8,256]{2,1,0:T(8,128)}, u32[]{:S(2)}, u32[]{:S(2)}) async-start(f32[128,8,256]{2,1,0:T(8,128)} %copy.73), calls=%async_computation.3 | async-start | bytes 2097152 | tf_op jit(solution)/shard_map/all_to_all | solution.py:29
  250.0 3.3 convolution_bitcast_fusion.1
  253.4 3.6 convolution_bitcast_fusion
  258.6 3.4 convolution_add_fusion.1
  261.9 181.6 %all-reduce.5.cloned.1.call-done = f32[1,256,1024]{2,1,0:T(8,128)} async-done(((f32[1,256,1024]{2,1,0:T(8,128)}), f32[1,256,1024]{2,1,0:T(8,128)}) %all-reduce.5.cloned.1.call-update) | async-done | bytes 1048592
  443.6 1.4 constant_dynamic-slice_fusion
  444.9 3.6 convolution_bitcast_fusion.6
  448.6 4.2 convolution_bitcast_fusion.2
  452.8 4.4 convolution_bitcast_fusion.3
  457.2 2.6 copy.76
  459.7 2.9 fusion.10
  462.7 121.8 %reduce-scatter.3.cloned.1.call-done = f32[1,16,256]{2,1,0:T(8,128)} async-done(((f32[1,1024,256]{2,1,0:T(8,128)}), f32[1,16,256]{2,1,0:T(8,128)}) %reduce-scatter.3.cloned.1.call-update) | async-done | bytes 16400 | tf_op jit(solution)/shard_map/reduce_scatter | solution.py:64
  584.5 123.4 %all-reduce.7.cloned.1.call-done = (f32[512,512]{1,0:T(8,128)}, f32[128,128]{1,0:T(8,128)}) async-done(((f32[512,512]{1,0:T(8,128)}, f32[128,128]{1,0:T(8,128)}), (f32[512,512]{1,0:T(8,128)}, f32[128,128]{1,0:T(8,128)})) %all-reduce.7.cloned.1.call-update) | async-done | bytes 1114128 | tf_op jit(solution)/shard_map/psum | solution.py:75
  707.8 2.3 copy.110
  710.1 1.5 copy.111
  (41 shorter events, 2.2 us)
Async XLA Ops:
  8.0 1.2 copy-start
  9.2 44.9 %copy-start.9 = (f32[128,128]{1,0:T(8,128)S(1)}, f32[128,128]{1,0:T(8,128)}, u32[]{:S(2)}) copy-start(f32[128,128]{1,0:T(8,128)} %param.10) | copy-start | bytes 196612
  14.5 51.1 %copy-start.12 = (bf16[1,4,1024]{2,1,0:T(4,128)(2,1)S(1)}, bf16[1,4,1024]{2,1,0:T(4,128)(2,1)}, u32[]{:S(2)}) copy-start(bf16[1,4,1024]{2,1,0:T(4,128)(2,1)} %param.11) | copy-start | bytes 24580
  53.1 1.0 copy-start.4
  53.1 85.3 %copy-start.11 = (bf16[1,16,256]{2,1,0:T(8,128)(2,1)S(1)}, bf16[1,16,256]{2,1,0:T(8,128)(2,1)}, u32[]{:S(2)}) copy-start(bf16[1,16,256]{2,1,0:T(8,128)(2,1)} %param.12) | copy-start | bytes 24580
  56.0 136.5 %copy-start.1 = (f32[1024,256]{1,0:T(8,128)S(1)}, f32[1024,256]{1,0:T(8,128)}, u32[]{:S(2)}) copy-start(f32[1024,256]{1,0:T(8,128)} %param.7) | copy-start | bytes 3145732
  57.4 134.0 %all-to-all-start.1 = ((f32[128,8,256]{2,1,0:T(8,128)}), f32[128,8,256]{2,1,0:T(8,128)S(1)}, u32[]{:S(2)}, u32[]{:S(2)}) async-start(f32[128,8,256]{2,1,0:T(8,128)} %copy.68), calls=%async_computation.1 | async-start | bytes 2097152 | tf_op jit(solution)/shard_map/all_to_all | solution.py:29
  191.5 1.6 copy-start.6
  191.6 1.0 copy-start.2
  193.1 2.4 copy-start.8
  193.1 2.4 copy-start.13
  197.6 1.8 copy-start.7
  235.1 1.1 copy-start.5
  241.7 206.9 %all-to-all-start.3 = ((f32[128,8,256]{2,1,0:T(8,128)}), f32[128,8,256]{2,1,0:T(8,128)}, u32[]{:S(2)}, u32[]{:S(2)}) async-start(f32[128,8,256]{2,1,0:T(8,128)} %copy.73), calls=%async_computation.3 | async-start | bytes 2097152 | tf_op jit(solution)/shard_map/all_to_all | solution.py:29
  250.0 193.6 %all-reduce.5.cloned.1.call-start = ((), (), s32[]{:S(2)}) async-start(), calls=%async_computation.6 | async-start | bytes 2097152
  253.3 4.0 copy-start.14
  253.4 331.1 %reduce-scatter.3.cloned.1.call-start = ((), (), s32[]{:S(2)}) async-start(), calls=%async_computation.5 | async-start | bytes 1064960 | tf_op jit(solution)/shard_map/reduce_scatter | solution.py:64
  257.0 450.8 %all-reduce.7.cloned.1.call-start = ((), (), s32[]{:S(2)}) async-start(), calls=%async_computation.7 | async-start | bytes 2228224 | tf_op jit(solution)/shard_map/psum | solution.py:75
  258.5 190.0 %copy-start.10 = (f32[2,512]{1,0:T(2,128)S(1)}, f32[2,512]{1,0:T(2,128)}, u32[]{:S(2)}) copy-start(f32[2,512]{1,0:T(2,128)} %param.9) | copy-start | bytes 12292
  448.6 11.2 %copy-start.3 = (f32[2,64,8,256]{3,2,1,0:T(8,128)S(1)}, f32[2,64,8,256]{3,2,1,0:T(8,128)}, u32[]{:S(2)}) copy-start(f32[2,64,8,256]{3,2,1,0:T(8,128)} %copy-done.2) | copy-start | bytes 3145732
Sparse Core Ops, SparseCore 0:
  255.2 188.3 all-reduce.4
  448.1 136.2 reduce-scatter.2
Sparse Core Ops, SparseCore 1:
  452.9 254.9 all-reduce.6
where the time goes:
time: 720 us; the launch traced here: 719 us
  waiting for transfers between devices  427 us (59%)
  blocking collectives  200 us (28%)
  matrix products  38.3 us (5%)
  local copies, waits for them, and re-layouts  17.5 us (2%)
  starting transfers between devices  16.7 us (2%)
  between operations  16.3 us (2%)
    unnamed x4, waiting for transfers between devices  182 us
    psum x1, waiting for transfers between devices, local(): grad_one, grad_two = lax.psum((one_part, two_part), ('tok', 'ch'))  123 us
    reduce_scatter x1, waiting for transfers between devices, local(): lax.psum_scatter(grad_down_part[None], 'tok', scatter_dimension=1, tiled=...  122 us
    all_to_all x2, blocking collectives, to_columns(): lax.all_to_all(block.reshape(rows, count, width // count, chans), 'tok',...  74.2 us
    all_gather x1, blocking collectives, local(): lax.all_gather(w_up, 'tok', axis=1, tiled=True)  72.8 us
    all_gather x1, blocking collectives, local(): lax.all_gather(w_down, 'tok', axis=1, tiled=True)  53.1 us
    all_to_all x2, starting transfers between devices, to_rows(): return lax.all_to_all(block, 'tok', split_axis=0, concat_axis=1, tiled=True)  16.4 us
  transfers between devices with their start and end apart: 5, of which 3 were waited for; matrix products, arithmetic and copies ran while one was open for 4% of the time, Pallas kernels for 0%

commit v1 on v0

--- a/solution.py
+++ b/solution.py
@@ -6,6 +6,9 @@
 
 inv_root_two = 1.0 / math.sqrt(2.0)
 inv_root_tau = 1.0 / math.sqrt(2.0 * math.pi)
+_proceed_seats_all = lambda q_in, axis_key, shard_axis: lax.psum(
+    lax.psum(q_in, axis_key), shard_axis
+)
 
 
 def gelu_parts(value):
@@ -72,7 +75,7 @@
     one_part = jnp.einsum("ikc,ijc->kj", d_first, grid, precision=high)
     d_grid = jnp.einsum("kj,ikc->ijc", factor_one, d_first, precision=high)
     grad_inputs = direct + d_grid.reshape(rows * width, chans)
-    grad_one, grad_two = lax.psum((one_part, two_part), ("tok", "ch"))
+    grad_one, grad_two = _proceed_seats_all((one_part, two_part), "ch", "tok")
     return (outputs, grad_inputs, grad_one, grad_two, grad_up, grad_down)
 
 

time: 720 us -> 679 us (0.943)
  waiting for transfers between devices: 427 us -> 387 us
    unnamed x4 -> x3, waiting for transfers between devices: 182 us -> 0.05 us
    psum x1 -> x2, waiting for transfers between devices: 123 us -> 223 us  [the longest x1 176 us: lax.psum(lax.psum(q_in, axis_key), shard_axis)]
    all_to_all x2, waiting for transfers between devices: 0.01 us -> 22.7 us  [to_rows(): return lax.all_to_all(block, 'tok', split_axis=0, concat_axis=1, tiled=True)]
    reduce_scatter x1, waiting for transfers between devices: 122 us -> 141 us  [local(): lax.psum_scatter(grad_down_part[None], 'tok', scatter_dimension=1, tiled=...]
  transfers between devices with their start and end apart: 5 -> 5, of which waited for: 3 -> 4; matrix products, arithmetic and copies ran while one was open for 4% -> 4% of each run, Pallas kernels for 0% -> 0%
where the time goes in v1:
time: 679 us; the launch traced here: 678 us
  waiting for transfers between devices  387 us (57%)
  blocking collectives  200 us (29%)
  matrix products  38.3 us (6%)
  local copies, waits for them, and re-layouts  17.4 us (3%)
  starting transfers between devices  16.7 us (2%)
  between operations  14.6 us (2%)
    psum x1, waiting for transfers between devices, lax.psum(lax.psum(q_in, axis_key), shard_axis)  176 us
    reduce_scatter x1, waiting for transfers between devices, local(): lax.psum_scatter(grad_down_part[None], 'tok', scatter_dimension=1, tiled=...  141 us
    all_to_all x2, blocking collectives, to_columns(): lax.all_to_all(block.reshape(rows, count, width // count, chans), 'tok',...  74.5 us
    all_gather x1, blocking collectives, local(): lax.all_gather(w_up, 'tok', axis=1, tiled=True)  72.8 us
    all_gather x1, blocking collectives, local(): lax.all_gather(w_down, 'tok', axis=1, tiled=True)  53 us
    psum x1, waiting for transfers between devices, lax.psum(q_in, axis_key)  47.1 us
    all_to_all x2, waiting for transfers between devices, to_rows(): return lax.all_to_all(block, 'tok', split_axis=0, concat_axis=1, tiled=True)  22.7 us
    all_to_all x2, starting transfers between devices, to_rows(): return lax.all_to_all(block, 'tok', split_axis=0, concat_axis=1, tiled=True)  16.4 us
  transfers between devices with their start and end apart: 5, of which 4 were waited for; matrix products, arithmetic and copies ran while one was open for 4% of the time, Pallas kernels for 0%

profile of v1, /device:TPU:4, one launch (start us, length us, event | category | flops | bytes accessed | tf_op | source)
XLA Modules:
  0.0 677.7 jit_solution(5887727596190054974)
XLA Ops:
  7.2 1.2 copy-done
  8.4 4.7 fusion.6
  13.6 38.7 %all_to_all.63 = f32[2,64,8,256]{3,2,0,1:T(8,128)S(1)} all-to-all(f32[2,64,8,256]{3,2,0,1:T(8,128)S(1)} %copy.66), channel_id=1, replica_groups=mesh['tok'=64,'ch'=4] {'tok'}, dimensions={1} | all-to-all | bytes 2097152 | tf_op jit(solution)/shard_map/all_to_all | solution.py:22
  52.3 1.0 copy-done.4
  53.3 1.9 convolution_bitcast_fusion.5
  55.2 1.4 copy.68
  56.6 8.1 %all-to-all-start.1 = ((f32[128,8,256]{2,1,0:T(8,128)}), f32[128,8,256]{2,1,0:T(8,128)S(1)}, u32[]{:S(2)}, u32[]{:S(2)}) async-start(f32[128,8,256]{2,1,0:T(8,128)} %copy.68), calls=%async_computation.1 | async-start | bytes 2097152 | tf_op jit(solution)/shard_map/all_to_all | solution.py:32
  64.7 72.8 %all_gather.6 = bf16[1,256,1024]{2,0,1:T(2,128)(2,1)} all-gather(bf16[1,4,1024]{2,0,1:T(2,128)(2,1)S(1)} %copy.70), channel_id=1, replica_groups=mesh['tok'=64,'ch'=4] {'tok'}, dimensions={1}, use_global_device_ids=true | all-gather | bytes 532480 | tf_op jit(solution)/shard_map/all_gather | solution.py:41
  137.6 53.0 %all_gather.7 = bf16[1,1024,256]{2,1,0:T(8,128)(2,1)} all-gather(bf16[1,16,256]{2,1,0:T(8,128)(2,1)S(1)} %copy-done.11), channel_id=1, replica_groups=mesh['tok'=64,'ch'=4] {'tok'}, dimensions={1}, use_global_device_ids=true | all-gather | bytes 532480 | tf_op jit(solution)/shard_map/all_gather | solution.py:42
  190.6 1.0 copy-done.2
  192.1 2.4 multiply_convert_fusion
  194.5 2.2 fusion.5
  196.7 1.8 fusion.33
  198.6 35.8 %all_to_all.64 = f32[2,64,8,256]{3,2,0,1:T(8,128)S(1)} all-to-all(f32[2,64,8,256]{3,2,0,1:T(8,128)S(1)} %copy.71), channel_id=1, replica_groups=mesh['tok'=64,'ch'=4] {'tok'}, dimensions={1} | all-to-all | bytes 2097152 | tf_op jit(solution)/shard_map/all_to_all | solution.py:22
  235.4 2.9 convolution_bitcast_fusion.4
  238.3 2.6 copy.73
  240.9 8.3 %all-to-all-start.3 = ((f32[128,8,256]{2,1,0:T(8,128)}), f32[128,8,256]{2,1,0:T(8,128)}, u32[]{:S(2)}, u32[]{:S(2)}) async-start(f32[128,8,256]{2,1,0:T(8,128)} %copy.73), calls=%async_computation.3 | async-start | bytes 2097152 | tf_op jit(solution)/shard_map/all_to_all | solution.py:32
  249.4 3.6 convolution_bitcast_fusion.6
  253.1 22.7 %all-to-all-done.3 = f32[128,8,256]{2,1,0:T(8,128)} async-done(((f32[128,8,256]{2,1,0:T(8,128)}), f32[128,8,256]{2,1,0:T(8,128)}, u32[]{:S(2)}, u32[]{:S(2)}) %all-to-all-start.3) | async-done | bytes 1048608 | tf_op jit(solution)/shard_map/all_to_all | solution.py:32
  275.7 4.1 convolution_bitcast_fusion.2
  279.9 3.3 convolution_bitcast_fusion.1
  283.2 47.1 %all-reduce.8.cloned.1.call-done = (f32[512,512]{1,0:T(8,128)}, f32[128,128]{1,0:T(8,128)}) async-done(((f32[512,512]{1,0:T(8,128)}, f32[128,128]{1,0:T(8,128)}), (f32[512,512]{1,0:T(8,128)}, f32[128,128]{1,0:T(8,128)})) %all-reduce.8.cloned.1.call-update) | async-done | bytes 1114128 | tf_op jit(solution)/shard_map/psum | solution.py:10
  330.4 3.7 convolution_bitcast_fusion
  335.3 3.4 convolution_add_fusion.1
  338.7 4.5 convolution_bitcast_fusion.3
  343.2 2.6 copy.76
  345.8 2.9 fusion.10
  348.7 175.9 %all-reduce.6.cloned.1.call-done = (f32[512,512]{1,0:T(8,128)}, f32[128,128]{1,0:T(8,128)}, f32[1,256,1024]{2,1,0:T(8,128)}) async-done(((f32[512,512]{1,0:T(8,128)}, f32[128,128]{1,0:T(8,128)}, f32[1,256,1024]{2,1,0:T(8,128)}), (f32[512,512]{1,0:T(8,128)}, f32[128,128]{1,0:T(8,128)}, f32[1,256,1024]{2,1,0:T(8,128)})) %all-reduce.6.cloned.1.call-update) | async-done | bytes 2162704 | tf_op jit(solution)/shard_map/psum | solution.py:9
  524.6 1.4 constant_dynamic-slice_fusion
  526.0 141.4 %reduce-scatter.3.cloned.1.call-done = f32[1,16,256]{2,1,0:T(8,128)} async-done(((f32[1,1024,256]{2,1,0:T(8,128)}), f32[1,16,256]{2,1,0:T(8,128)}) %reduce-scatter.3.cloned.1.call-update) | async-done | bytes 16400 | tf_op jit(solution)/shard_map/reduce_scatter | solution.py:67
  667.4 2.3 copy.112
  669.7 1.5 copy.113
  (41 shorter events, 3.2 us)
Async XLA Ops:
  7.2 1.2 copy-start
  8.4 44.9 %copy-start.9 = (f32[128,128]{1,0:T(8,128)S(1)}, f32[128,128]{1,0:T(8,128)}, u32[]{:S(2)}) copy-start(f32[128,128]{1,0:T(8,128)} %param.10) | copy-start | bytes 196612
  13.6 51.1 %copy-start.12 = (bf16[1,4,1024]{2,1,0:T(4,128)(2,1)S(1)}, bf16[1,4,1024]{2,1,0:T(4,128)(2,1)}, u32[]{:S(2)}) copy-start(bf16[1,4,1024]{2,1,0:T(4,128)(2,1)} %param.11) | copy-start | bytes 24580
  52.3 1.0 copy-start.4
  52.3 85.3 %copy-start.11 = (bf16[1,16,256]{2,1,0:T(8,128)(2,1)S(1)}, bf16[1,16,256]{2,1,0:T(8,128)(2,1)}, u32[]{:S(2)}) copy-start(bf16[1,16,256]{2,1,0:T(8,128)(2,1)} %param.12) | copy-start | bytes 24580
  55.2 136.4 %copy-start.1 = (f32[1024,256]{1,0:T(8,128)S(1)}, f32[1024,256]{1,0:T(8,128)}, u32[]{:S(2)}) copy-start(f32[1024,256]{1,0:T(8,128)} %param.7) | copy-start | bytes 3145732
  56.6 133.9 %all-to-all-start.1 = ((f32[128,8,256]{2,1,0:T(8,128)}), f32[128,8,256]{2,1,0:T(8,128)S(1)}, u32[]{:S(2)}, u32[]{:S(2)}) async-start(f32[128,8,256]{2,1,0:T(8,128)} %copy.68), calls=%async_computation.1 | async-start | bytes 2097152 | tf_op jit(solution)/shard_map/all_to_all | solution.py:32
  190.5 1.6 copy-start.6
  190.6 1.0 copy-start.2
  192.1 2.4 copy-start.8
  192.1 2.4 copy-start.13
  196.7 1.8 copy-start.7
  234.4 1.0 copy-start.5
  235.4 40.3 %copy-start.10 = (f32[2,512]{1,0:T(2,128)S(1)}, f32[2,512]{1,0:T(2,128)}, u32[]{:S(2)}) copy-start(f32[2,512]{1,0:T(2,128)} %param.9) | copy-start | bytes 12292
  240.9 34.9 %all-to-all-start.3 = ((f32[128,8,256]{2,1,0:T(8,128)}), f32[128,8,256]{2,1,0:T(8,128)}, u32[]{:S(2)}, u32[]{:S(2)}) async-start(f32[128,8,256]{2,1,0:T(8,128)} %copy.73), calls=%async_computation.3 | async-start | bytes 2097152 | tf_op jit(solution)/shard_map/all_to_all | solution.py:32
  249.2 81.1 %all-reduce.8.cloned.1.call-start = ((), (), s32[]{:S(2)}) async-start(), calls=%async_computation.7 | async-start | bytes 2228224 | tf_op jit(solution)/shard_map/psum | solution.py:10
  279.9 244.8 %all-reduce.6.cloned.1.call-start = ((), (), s32[]{:S(2)}) async-start(), calls=%async_computation.6 | async-start | bytes 4325376 | tf_op jit(solution)/shard_map/psum | solution.py:9
  330.3 3.8 copy-start.14
  330.3 337.1 %reduce-scatter.3.cloned.1.call-start = ((), (), s32[]{:S(2)}) async-start(), calls=%async_computation.5 | async-start | bytes 1064960 | tf_op jit(solution)/shard_map/reduce_scatter | solution.py:67
  338.7 7.1 %copy-start.3 = (f32[2,64,8,256]{3,2,1,0:T(8,128)S(1)}, f32[2,64,8,256]{3,2,1,0:T(8,128)}, u32[]{:S(2)}) copy-start(f32[2,64,8,256]{3,2,1,0:T(8,128)} %copy-done.2) | copy-start | bytes 3145732
Sparse Core Ops, SparseCore 0:
  280.0 50.2 all-reduce.7
  334.4 190.1 all-reduce.5
  529.7 137.6 reduce-scatter.2
